TPU v7x, 32 devices: a whole 2x2x4 slice. The times are simulated.
32 devices in a mesh: row: 4 (over x, core), col: 8 (over z, y).
Axes of the slice: x: 2, y: 2, z: 4, core: 2. Of those that a mesh axis runs over, the one named last changes fastest.
Arguments:
- x_vals: bfloat16 [256, 32, 4096], P(('row', 'col')), may hold values from -6 to 6
- occupancy: int32 [256, 32], P(('row', 'col')), may hold values from 0 to 1, as said below
- perm: int32 [256], replicated, may hold values from 0 to 255, as said below
Outputs:
- sign_iterate_next: bfloat16 [16384, 16384], P('row', 'col')
Inputs may be any that keep to these rules, and one draw needn't show every extreme that they name: occupancy[i, s] = 1 marks block (i, (i - 16 + s) mod 256) as present; the diagonal slot s = 16 is always 1, and some row has all 32 slots 1. perm is a permutation with perm[j] = a(j mod (8)) * 32 + b(j div (8)) for permutations a and b; so the 32 band columns of any row fall exactly 4 times into each aligned run of 32 new indices, and each aligned run of 64 initial indices has exactly 16 members in each aligned run of 64 new indices.
All inputs are finite; a program needn't handle non-finite values.
Results may differ from a plain program's by a relative error of at most 0.0017.
Values may be sent and summed in bfloat16 or wider, within the bound.
A program may use at most 128 MiB of HBM per device.

v0:
```python
import math

import jax
import jax.numpy as jnp
from jax import lax
from jax.sharding import PartitionSpec as P

BLOCK_EDGE = 64


def bucket_slots(x_vals, occupancy, perm, first_row, column_processors, tile_slots):
    local_rows, band_extent = occupancy.shape
    block_count = perm.shape[0]
    panel_cols = block_count // column_processors
    row_ids = first_row + jnp.arange(local_rows, dtype=jnp.int32)
    orig_cols = (
        row_ids[:, None] - band_extent // 2 + jnp.arange(band_extent, dtype=jnp.int32)[None, :]
    ) % block_count
    new_cols = perm[orig_cols]
    panel_of = new_cols // panel_cols
    inside = new_cols % panel_cols
    in_panel = (
        (occupancy[:, :, None] == 1)
        & (panel_of[:, :, None] == jnp.arange(column_processors)[None, None, :])
    ).astype(jnp.int32)
    before = jnp.cumsum(in_panel, axis=1) - in_panel
    slot_rank = jnp.sum(before * in_panel, axis=2)
    placed = in_panel[:, :, :, None] * (
        slot_rank[:, :, None, None] == jnp.arange(tile_slots)[None, None, None, :]
    ).astype(jnp.int32)
    values = jnp.einsum(
        "kspt,ksf->pktf", placed.astype(jnp.bfloat16), x_vals, preferred_element_type=jnp.float32
    ).astype(jnp.bfloat16)
    columns = jnp.einsum("kspt,ks->pkt", placed, inside + 1) - 1
    return (values, columns)


def filtered_product(row_vals, row_cols, far_vals, far_cols, tile_cols, panel_cols):
    panel_rows, tile_slots = tile_cols.shape
    panel_count = row_vals.shape[0]
    block_area = row_vals.shape[3]
    group = math.gcd(panel_count, max(1, 16 // (tile_slots * tile_slots)))
    wanted = tile_cols >= 0

    def one_group(running, inputs):
        panel_index, piece_vals, piece_cols = inputs
        present_mask = piece_cols >= 0
        source = jnp.where(present_mask, panel_index[:, None, None] * panel_cols + piece_cols, 0)
        found_cols = far_cols[source]
        whole_rows = far_vals[source]
        chosen = jnp.zeros((group, panel_rows, tile_slots, tile_slots, block_area), far_vals.dtype)
        for slot in range(tile_slots):
            hit = (
                (found_cols[:, :, :, slot][:, :, :, None] == tile_cols[None, :, None, :])
                & present_mask[:, :, :, None]
                & wanted[None, :, None, :]
            )
            chosen = jnp.where(
                hit[:, :, :, :, None], whole_rows[:, :, :, slot][:, :, :, None, :], chosen
            )
        left_factor_blocks = piece_vals.reshape(
            group, panel_rows, tile_slots, BLOCK_EDGE, BLOCK_EDGE
        )
        right_factor_blocks = chosen.reshape(
            group, panel_rows, tile_slots, tile_slots, BLOCK_EDGE, BLOCK_EDGE
        )
        update = jnp.einsum(
            "givab,givubc->iuac",
            left_factor_blocks,
            right_factor_blocks,
            preferred_element_type=jnp.float32,
        )
        return (running + update, None)

    start = jnp.zeros((panel_rows, tile_slots, BLOCK_EDGE, BLOCK_EDGE), jnp.float32)
    panel_ids = jnp.arange(panel_count, dtype=jnp.int32).reshape(panel_count // group, group)
    grouped_vals = row_vals.reshape(panel_count // group, group, panel_rows, tile_slots, block_area)
    grouped_cols = row_cols.reshape(panel_count // group, group, panel_rows, tile_slots)
    running, _ = lax.scan(one_group, start, (panel_ids, grouped_vals, grouped_cols))
    return running.reshape(panel_rows, tile_slots, BLOCK_EDGE * BLOCK_EDGE)


def shards(x_vals, occupancy, perm):
    row_devices = lax.axis_size("row")
    column_processors = lax.axis_size("col")
    own_row = lax.axis_index("row")
    own_col = lax.axis_index("col")
    local_rows = x_vals.shape[0]
    band_extent = x_vals.shape[1]
    block_area = x_vals.shape[2]
    block_count = perm.shape[0]
    panel_rows = block_count // row_devices
    panel_cols = block_count // column_processors
    tile_slots = band_extent // column_processors
    first_row = (own_row * column_processors + own_col) * local_rows
    values, columns = bucket_slots(
        x_vals, occupancy, perm, first_row, column_processors, tile_slots
    )
    first_vals, first_cols = (
        lax.all_to_all(values, "col", split_axis=0, concat_axis=0, tiled=True),
        lax.all_to_all(
            columns.astype(jnp.bfloat16), "col", split_axis=0, concat_axis=0, tiled=True
        ),
    )
    first_vals = first_vals.reshape(panel_rows, tile_slots, block_area)
    first_cols = first_cols.astype(jnp.int32).reshape(panel_rows, tile_slots)
    group_new = lax.dynamic_slice_in_dim(perm, own_row * panel_rows, panel_rows) // panel_rows
    per_panel = panel_rows // row_devices
    heading = (group_new[:, None] == jnp.arange(row_devices)[None, :]).astype(jnp.int32)
    ahead = jnp.cumsum(heading, axis=0) - heading
    order_in = jnp.sum(ahead * heading, axis=1)
    placed = heading[:, :, None] * (
        order_in[:, None, None] == jnp.arange(per_panel)[None, None, :]
    ).astype(jnp.int32)
    send_vals = jnp.einsum(
        "gre,gtf->retf", placed.astype(jnp.bfloat16), first_vals, preferred_element_type=jnp.float32
    ).astype(jnp.bfloat16)
    send_cols = (jnp.einsum("gre,gt->ret", placed, first_cols + 1) - 1).astype(jnp.bfloat16)
    got_vals, got_cols = (
        lax.all_to_all(send_vals, "row", split_axis=0, concat_axis=0, tiled=True),
        lax.all_to_all(send_cols, "row", split_axis=0, concat_axis=0, tiled=True),
    )
    got_vals = got_vals.reshape(panel_rows, tile_slots * block_area)
    got_cols = got_cols.astype(jnp.int32).reshape(panel_rows, tile_slots)
    every_new = perm.reshape(row_devices, panel_rows)
    landing = (every_new // panel_rows == own_row).astype(jnp.int32)
    earlier = jnp.cumsum(landing, axis=1) - landing
    arrival = landing[:, :, None] * (
        earlier[:, :, None] == jnp.arange(per_panel)[None, None, :]
    ).astype(jnp.int32)
    target_row = (
        (every_new - own_row * panel_rows)[:, :, None] == jnp.arange(panel_rows)[None, None, :]
    ).astype(jnp.int32)
    selector = jnp.einsum("sge,sgl->lse", arrival, target_row).reshape(panel_rows, panel_rows)
    tile_vals = jnp.dot(
        selector.astype(jnp.bfloat16), got_vals, preferred_element_type=jnp.float32
    ).astype(jnp.bfloat16)
    tile_vals = tile_vals.reshape(panel_rows, tile_slots, block_area)
    tile_cols = jnp.dot(selector, got_cols + 1) - 1
    cols_wire = tile_cols.astype(jnp.bfloat16)
    row_vals, row_cols = (
        lax.all_gather(tile_vals[None], "col", axis=0, tiled=True),
        lax.all_gather(cols_wire[None], "col", axis=0, tiled=True),
    )
    row_cols = row_cols.astype(jnp.int32)
    far_vals, far_cols = (
        lax.all_gather(tile_vals, "row", axis=0, tiled=True),
        lax.all_gather(cols_wire, "row", axis=0, tiled=True),
    )
    far_cols = far_cols.astype(jnp.int32)
    square = filtered_product(row_vals, row_cols, far_vals, far_cols, tile_cols, panel_cols).astype(
        jnp.bfloat16
    )
    far_square = lax.all_gather(square, "row", axis=0, tiled=True)
    cube_vals = filtered_product(row_vals, row_cols, far_square, far_cols, tile_cols, panel_cols)
    stepped_matrix = (
        1.5 * tile_vals.astype(jnp.float32) - 0.5 / (BLOCK_EDGE * band_extent) * cube_vals
    )
    spread = (tile_cols[:, :, None] == jnp.arange(panel_cols)[None, None, :]).astype(jnp.float32)
    dense_tile = jnp.einsum(
        "iuj,iuac->iajc",
        spread,
        stepped_matrix.reshape(panel_rows, tile_slots, BLOCK_EDGE, BLOCK_EDGE),
    )
    return dense_tile.reshape(panel_rows * BLOCK_EDGE, panel_cols * BLOCK_EDGE).astype(jnp.bfloat16)


def solution(mesh):
    return jax.shard_map(
        shards,
        mesh=mesh,
        in_specs=(P(("row", "col"), None, None), P(("row", "col"), None), P()),
        out_specs=P("row", "col"),
        check_vma=False,
    )
```

profile of v0, /device:TPU:0, one launch (start us, length us, event | category | flops | bytes accessed | tf_op | source)
XLA Modules:
  0.0 2926.8 jit_solution(10407044865748420455)
XLA Ops:
  21.5 47.9 %all-to-all-done = bf16[8,8,4,4096]{3,2,1,0:T(4,128)(2,1)} async-done(((bf16[8,8,4,4096]{3,2,1,0:T(4,128)(2,1)}), bf16[8,8,4,4096]{3,2,1,0:T(4,128)(2,1)}, u32[]{:S(2)}, u32[]{:S(2)}) %all-to-all-start) | async-done | bytes 2097184 | tf_op jit(solution)/shard_map/all_to_all | solution.py:100
  80.5 24.8 all-to-all-done.1
  144.5 17.9 all-gather.1
  167.9 177.1 %all-gather.9.cloned.1.call-done = bf16[8,64,4,4096]{3,1,2,0:T(8,128)(2,1)} async-done(((bf16[1,64,4,4096]{3,1,2,0:T(8,128)(2,1)}), bf16[8,64,4,4096]{3,1,2,0:T(8,128)(2,1)}) %all-gather.9.cloned.1.call-update) | async-done | bytes 16777232 | tf_op jit(solution)/shard_map/all_gather | solution.py:142
  345.0 22.2 copy.185
  367.2 35.8 %all-gather.7.cloned.1.call-done = bf16[256,4,4096]{2,1,0:T(4,128)(2,1)} async-done(((bf16[64,4,4096]{2,1,0:T(4,128)(2,1)}), bf16[256,4,4096]{2,1,0:T(4,128)(2,1)}) %all-gather.7.cloned.1.call-update) | async-done | bytes 8388624 | tf_op jit(solution)/shard_map/all_gather | solution.py:147
  403.0 1186.5 %while.22 = (s32[]{:T(128)}, f32[64,4,64,64]{2,3,1,0:T(8,128)}, s32[8,1,64,4]{3,2,1,0:T(8,128)S(1)}, s32[8,1]{0,1:T(1,128)S(1)}, s32[256,4]{1,0:T(8,128)S(1)}, /...) while((s32[]{:T(128)}, f32[64,4,64,64]{2,3,1,0:T(8,128)}, ...), condition=%wide.region_6.7_spmd.clone, body=%wide.region_5.6_spmd.clone.sunk | while | flops 555760128 | bytes 94430096 | solution.py:79
  438.1 47.0 %slice_reduce_fusion.10 = (bf16[64,4,4096]{2,1,0:T(4,128)(2,1)}, bf16[64,4,4096]{2,1,0:T(4,128)(2,1)}, bf16[64,4,4096]{2,1,0:T(4,128)(2,1)}, bf16[64,4,4096]{2,1,0:T(4,128)(2,1)}) fusion(bf16[1,64,4,4,4096]{4,3,2,1,0:T(4,128)(2,1)} %bitcast.158), kind=kLoop, calls=%fused_computation.23.clone.1 | loop fusion | bytes 16777216 | tf_op jit(solution)/shard_map/while/body/eval_jaxpr/slice | solution.py:59
  566.9 16.1 gather_fusion.1
  583.0 47.0 %slice_reduce_fusion.10 = (bf16[64,4,4096]{2,1,0:T(4,128)(2,1)}, bf16[64,4,4096]{2,1,0:T(4,128)(2,1)}, bf16[64,4,4096]{2,1,0:T(4,128)(2,1)}, bf16[64,4,4096]{2,1,0:T(4,128)(2,1)}) fusion(bf16[1,64,4,4,4096]{4,3,2,1,0:T(4,128)(2,1)} %bitcast.158), kind=kLoop, calls=%fused_computation.23.clone.1 | loop fusion | bytes 16777216 | tf_op jit(solution)/shard_map/while/body/eval_jaxpr/slice | solution.py:59
  713.4 16.2 gather_fusion.1
  729.6 47.0 %slice_reduce_fusion.10 = (bf16[64,4,4096]{2,1,0:T(4,128)(2,1)}, bf16[64,4,4096]{2,1,0:T(4,128)(2,1)}, bf16[64,4,4096]{2,1,0:T(4,128)(2,1)}, bf16[64,4,4096]{2,1,0:T(4,128)(2,1)}) fusion(bf16[1,64,4,4,4096]{4,3,2,1,0:T(4,128)(2,1)} %bitcast.158), kind=kLoop, calls=%fused_computation.23.clone.1 | loop fusion | bytes 16777216 | tf_op jit(solution)/shard_map/while/body/eval_jaxpr/slice | solution.py:59
  860.0 16.2 gather_fusion.1
  876.1 47.0 %slice_reduce_fusion.10 = (bf16[64,4,4096]{2,1,0:T(4,128)(2,1)}, bf16[64,4,4096]{2,1,0:T(4,128)(2,1)}, bf16[64,4,4096]{2,1,0:T(4,128)(2,1)}, bf16[64,4,4096]{2,1,0:T(4,128)(2,1)}) fusion(bf16[1,64,4,4,4096]{4,3,2,1,0:T(4,128)(2,1)} %bitcast.158), kind=kLoop, calls=%fused_computation.23.clone.1 | loop fusion | bytes 16777216 | tf_op jit(solution)/shard_map/while/body/eval_jaxpr/slice | solution.py:59
  1022.6 47.0 %slice_reduce_fusion.10 = (bf16[64,4,4096]{2,1,0:T(4,128)(2,1)}, bf16[64,4,4096]{2,1,0:T(4,128)(2,1)}, bf16[64,4,4096]{2,1,0:T(4,128)(2,1)}, bf16[64,4,4096]{2,1,0:T(4,128)(2,1)}) fusion(bf16[1,64,4,4,4096]{4,3,2,1,0:T(4,128)(2,1)} %bitcast.158), kind=kLoop, calls=%fused_computation.23.clone.1 | loop fusion | bytes 16777216 | tf_op jit(solution)/shard_map/while/body/eval_jaxpr/slice | solution.py:59
  1153.0 16.2 gather_fusion.1
  1169.2 47.0 %slice_reduce_fusion.10 = (bf16[64,4,4096]{2,1,0:T(4,128)(2,1)}, bf16[64,4,4096]{2,1,0:T(4,128)(2,1)}, bf16[64,4,4096]{2,1,0:T(4,128)(2,1)}, bf16[64,4,4096]{2,1,0:T(4,128)(2,1)}) fusion(bf16[1,64,4,4,4096]{4,3,2,1,0:T(4,128)(2,1)} %bitcast.158), kind=kLoop, calls=%fused_computation.23.clone.1 | loop fusion | bytes 16777216 | tf_op jit(solution)/shard_map/while/body/eval_jaxpr/slice | solution.py:59
  1315.7 47.0 %slice_reduce_fusion.10 = (bf16[64,4,4096]{2,1,0:T(4,128)(2,1)}, bf16[64,4,4096]{2,1,0:T(4,128)(2,1)}, bf16[64,4,4096]{2,1,0:T(4,128)(2,1)}, bf16[64,4,4096]{2,1,0:T(4,128)(2,1)}) fusion(bf16[1,64,4,4,4096]{4,3,2,1,0:T(4,128)(2,1)} %bitcast.158), kind=kLoop, calls=%fused_computation.23.clone.1 | loop fusion | bytes 16777216 | tf_op jit(solution)/shard_map/while/body/eval_jaxpr/slice | solution.py:59
  1446.1 16.1 gather_fusion.1
  1462.2 47.0 %slice_reduce_fusion.10 = (bf16[64,4,4096]{2,1,0:T(4,128)(2,1)}, bf16[64,4,4096]{2,1,0:T(4,128)(2,1)}, bf16[64,4,4096]{2,1,0:T(4,128)(2,1)}, bf16[64,4,4096]{2,1,0:T(4,128)(2,1)}) fusion(bf16[1,64,4,4,4096]{4,3,2,1,0:T(4,128)(2,1)} %bitcast.158), kind=kLoop, calls=%fused_computation.23.clone.1 | loop fusion | bytes 16777216 | tf_op jit(solution)/shard_map/while/body/eval_jaxpr/slice | solution.py:59
  1626.1 41.7 %all-gather.11.cloned.1.call-done = bf16[256,4,4096]{2,1,0:T(4,128)(2,1)} async-done(((bf16[64,4,4096]{2,1,0:T(4,128)(2,1)}), bf16[256,4,4096]{2,1,0:T(4,128)(2,1)}) %all-gather.11.cloned.1.call-update) | async-done | bytes 8388624 | tf_op jit(solution)/shard_map/all_gather | solution.py:154
  1667.9 1172.5 %while.23 = (s32[]{:T(128)}, f32[64,4,64,64]{2,3,1,0:T(8,128)}, s32[8,1,64,4]{3,2,1,0:T(8,128)S(1)}, s32[8,1]{0,1:T(1,128)S(1)}, s32[256,4]{1,0:T(8,128)S(1)}, /...) while((s32[]{:T(128)}, f32[64,4,64,64]{2,3,1,0:T(8,128)}, ...), condition=%wide.region_8.9_spmd.clone, body=%wide.region_7.8_spmd.clone.sunk | while | flops 555760128 | bytes 94430096 | solution.py:79
  1687.6 47.3 %slice_reduce_fusion.11 = (bf16[64,4,4096]{2,1,0:T(4,128)(2,1)}, bf16[64,4,4096]{2,1,0:T(4,128)(2,1)}, bf16[64,4,4096]{2,1,0:T(4,128)(2,1)}, bf16[64,4,4096]{2,1,0:T(4,128)(2,1)}) fusion(bf16[1,64,4,4,4096]{4,3,2,1,0:T(4,128)(2,1)} %bitcast.159), kind=kLoop, calls=%fused_computation.53.clone.1 | loop fusion | bytes 16777216 | tf_op jit(solution)/shard_map/while/body/eval_jaxpr/slice | solution.py:59
  1832.8 47.3 %slice_reduce_fusion.11 = (bf16[64,4,4096]{2,1,0:T(4,128)(2,1)}, bf16[64,4,4096]{2,1,0:T(4,128)(2,1)}, bf16[64,4,4096]{2,1,0:T(4,128)(2,1)}, bf16[64,4,4096]{2,1,0:T(4,128)(2,1)}) fusion(bf16[1,64,4,4,4096]{4,3,2,1,0:T(4,128)(2,1)} %bitcast.159), kind=kLoop, calls=%fused_computation.53.clone.1 | loop fusion | bytes 16777216 | tf_op jit(solution)/shard_map/while/body/eval_jaxpr/slice | solution.py:59
  1979.5 47.3 %slice_reduce_fusion.11 = (bf16[64,4,4096]{2,1,0:T(4,128)(2,1)}, bf16[64,4,4096]{2,1,0:T(4,128)(2,1)}, bf16[64,4,4096]{2,1,0:T(4,128)(2,1)}, bf16[64,4,4096]{2,1,0:T(4,128)(2,1)}) fusion(bf16[1,64,4,4,4096]{4,3,2,1,0:T(4,128)(2,1)} %bitcast.159), kind=kLoop, calls=%fused_computation.53.clone.1 | loop fusion | bytes 16777216 | tf_op jit(solution)/shard_map/while/body/eval_jaxpr/slice | solution.py:59
  2126.2 47.3 %slice_reduce_fusion.11 = (bf16[64,4,4096]{2,1,0:T(4,128)(2,1)}, bf16[64,4,4096]{2,1,0:T(4,128)(2,1)}, bf16[64,4,4096]{2,1,0:T(4,128)(2,1)}, bf16[64,4,4096]{2,1,0:T(4,128)(2,1)}) fusion(bf16[1,64,4,4,4096]{4,3,2,1,0:T(4,128)(2,1)} %bitcast.159), kind=kLoop, calls=%fused_computation.53.clone.1 | loop fusion | bytes 16777216 | tf_op jit(solution)/shard_map/while/body/eval_jaxpr/slice | solution.py:59
  2272.9 47.3 %slice_reduce_fusion.11 = (bf16[64,4,4096]{2,1,0:T(4,128)(2,1)}, bf16[64,4,4096]{2,1,0:T(4,128)(2,1)}, bf16[64,4,4096]{2,1,0:T(4,128)(2,1)}, bf16[64,4,4096]{2,1,0:T(4,128)(2,1)}) fusion(bf16[1,64,4,4,4096]{4,3,2,1,0:T(4,128)(2,1)} %bitcast.159), kind=kLoop, calls=%fused_computation.53.clone.1 | loop fusion | bytes 16777216 | tf_op jit(solution)/shard_map/while/body/eval_jaxpr/slice | solution.py:59
  2403.5 16.1 gather_fusion.3
  2419.6 47.3 %slice_reduce_fusion.11 = (bf16[64,4,4096]{2,1,0:T(4,128)(2,1)}, bf16[64,4,4096]{2,1,0:T(4,128)(2,1)}, bf16[64,4,4096]{2,1,0:T(4,128)(2,1)}, bf16[64,4,4096]{2,1,0:T(4,128)(2,1)}) fusion(bf16[1,64,4,4,4096]{4,3,2,1,0:T(4,128)(2,1)} %bitcast.159), kind=kLoop, calls=%fused_computation.53.clone.1 | loop fusion | bytes 16777216 | tf_op jit(solution)/shard_map/while/body/eval_jaxpr/slice | solution.py:59
  2566.3 47.3 %slice_reduce_fusion.11 = (bf16[64,4,4096]{2,1,0:T(4,128)(2,1)}, bf16[64,4,4096]{2,1,0:T(4,128)(2,1)}, bf16[64,4,4096]{2,1,0:T(4,128)(2,1)}, bf16[64,4,4096]{2,1,0:T(4,128)(2,1)}) fusion(bf16[1,64,4,4,4096]{4,3,2,1,0:T(4,128)(2,1)} %bitcast.159), kind=kLoop, calls=%fused_computation.53.clone.1 | loop fusion | bytes 16777216 | tf_op jit(solution)/shard_map/while/body/eval_jaxpr/slice | solution.py:59
  2713.0 47.3 %slice_reduce_fusion.11 = (bf16[64,4,4096]{2,1,0:T(4,128)(2,1)}, bf16[64,4,4096]{2,1,0:T(4,128)(2,1)}, bf16[64,4,4096]{2,1,0:T(4,128)(2,1)}, bf16[64,4,4096]{2,1,0:T(4,128)(2,1)}) fusion(bf16[1,64,4,4,4096]{4,3,2,1,0:T(4,128)(2,1)} %bitcast.159), kind=kLoop, calls=%fused_computation.53.clone.1 | loop fusion | bytes 16777216 | tf_op jit(solution)/shard_map/while/body/eval_jaxpr/slice | solution.py:59
  2873.8 46.0 %convert_element_type.138 = bf16[4096,2048]{1,0:T(8,128)(2,1)} reshape(bf16[64,64,32,64]{3,2,1,0:T(8,128)(2,1)} %convert_bitcast_fusion) | data formatting | bytes 33554432 | tf_op jit(solution)/shard_map/convert_element_type | solution.py:165
  (509 shorter events, 1631.5 us)
Async XLA Ops:
  6.5 3.6 copy-start
  6.5 2.3 copy-start.3
  10.8 10.3 copy-start.2
  13.8 55.6 %all-to-all-start = ((bf16[8,8,4,4096]{3,2,1,0:T(4,128)(2,1)}), bf16[8,8,4,4096]{3,2,1,0:T(4,128)(2,1)}, u32[]{:S(2)}, u32[]{:S(2)}) async-start(bf16[8,8,4,4096]{3,2,1,0:T(4,128)(2,1)} %copy.175), calls=%async_computation | async-start | bytes 4194304 | tf_op jit(solution)/shard_map/all_to_all | solution.py:100
  75.2 30.2 %all-to-all-start.1 = ((bf16[4,16,4,4096]{3,1,2,0:T(8,128)(2,1)}), bf16[4,16,4,4096]{3,1,2,0:T(8,128)(2,1)}, u32[]{:S(2)}, u32[]{:S(2)}) async-start(bf16[4,16,4,4096]{3,1,2,0:T(8,128)(2,1)} %convolution_convert_fusion.1), calls=%async_computation.1 | async-start | bytes 4194304 | tf_op jit(solution)/shard_map/all_to_all | solution.py:120
  79.6 265.4 %all-gather.9.cloned.1.call-start = ((), (), s32[]{:S(2)}) async-start(), calls=%async_computation.5 | async-start | bytes 18874368 | tf_op jit(solution)/shard_map/all_gather | solution.py:142
  119.4 283.6 %all-gather.7.cloned.1.call-start = ((), (), s32[]{:S(2)}) async-start(), calls=%async_computation.4 | async-start | bytes 10485760 | tf_op jit(solution)/shard_map/all_gather | solution.py:147
  137.2 7.0 all-to-all-start.3
  140.5 1527.4 %all-gather.11.cloned.1.call-start = ((), (), s32[]{:S(2)}) async-start(), calls=%async_computation.6 | async-start | bytes 10485760 | tf_op jit(solution)/shard_map/all_gather | solution.py:154
  2873.8 46.0 %copy-start.1 = (bf16[8,32,4096]{2,1,0:T(8,128)(2,1)S(1)}, bf16[8,32,4096]{2,1,0:T(8,128)(2,1)}, u32[]{:S(2)}) copy-start(bf16[8,32,4096]{2,1,0:T(8,128)(2,1)} %param.7) | copy-start | bytes 6291460
Sparse Core Ops, SparseCore 0:
  119.5 225.4 all-gather.8
  346.6 56.4 all-gather.6
  1609.6 58.2 all-gather.10
where the time goes:
time: 2960 us; the launch traced here: 2930 us
  local copies, waits for them, and re-layouts  2210 us (75%)
  waiting for transfers between devices  331 us (11%)
  matrix products  268 us (9%)
  other arithmetic  42.8 us (1%)
  blocking collectives  33.6 us (1%)
    broadcast_in_dim x128, local copies, waits for them, and re-layouts, one_group(): jnp.where(hit[:, :, :, :, None], whole_rows[:, :, :, slot][:, :, :, None,...  853 us
    slice x16, local copies, waits for them, and re-layouts, one_group(): whole_rows[:, :, :, slot][:, :, :, None, :]  755 us
    gather x16, local copies, waits for them, and re-layouts, one_group(): whole_rows = far_vals[source]  258 us
    dot_general x16, matrix products, one_group(): jnp.einsum('givab,givubc->iuac', left_factor_blocks, right_factor_blocks,...  238 us
    all_gather x1, waiting for transfers between devices, shards(): lax.all_gather(tile_vals[None], 'col', axis=0, tiled=True)  177 us
    another operation x16, local copies, waits for them, and re-layouts  112 us
    dynamic_slice x16, local copies, waits for them, and re-layouts, filtered_product(): lax.scan(one_group, start, (panel_ids, grouped_vals, grouped_cols))  72.1 us
  transfers between devices with their start and end apart: 6, of which 6 were waited for; matrix products, arithmetic and copies ran while one was open for 2% of the time, Pallas kernels for 0%

commit v1 on v0

v1 whole, which is shorter than its diff:
```python
import jax
import jax.numpy as jnp
from jax import lax
from jax.experimental import pallas as pl
from jax.experimental.pallas import tpu as pltpu
from jax.sharding import PartitionSpec as P

BLOCK_EDGE = 64


def multiply_kernel(order_ref, left_ref, far0, far1, far2, far3, out_ref):
    width = out_ref.shape[-1]
    left = left_ref[...].reshape(-1, width)
    right = jnp.concatenate([r[...].reshape(-1, width) for r in (far0, far1, far2, far3)], axis=0)
    update = jnp.dot(left, right, preferred_element_type=jnp.float32).reshape(out_ref.shape)

    @pl.when(pl.program_id(1) == 0)
    def _():
        out_ref[...] = update

    @pl.when(pl.program_id(1) != 0)
    def _():
        out_ref[...] += update


def banded_product(left, far, order, residue_major, slots):
    panels, halves, count, edge, width = left.shape
    chunk = slots // 2
    chunks = count // chunk

    def far_spec(position):
        def chunk_of(g):
            return lax.rem(2 * g + chunks - 1 + lax.rem(position + 1 + 2 * g, 4), chunks)

        if residue_major:
            return pl.BlockSpec(
                (1, chunk, edge, width), lambda g, p, order: (order[p], chunk_of(g), 0, 0)
            )
        return pl.BlockSpec(
            (chunk, 1, edge, width), lambda g, p, order: (chunk_of(g), order[p], 0, 0)
        )

    return pl.pallas_call(
        multiply_kernel,
        out_shape=jax.ShapeDtypeStruct((halves, count, edge, width), jnp.float32),
        grid_spec=pltpu.PrefetchScalarGridSpec(
            num_scalar_prefetch=1,
            grid=(count // slots, panels),
            in_specs=[
                pl.BlockSpec(
                    (1, halves, slots, edge, width), lambda g, p, order: (p, 0, g, 0, 0)
                )
            ]
            + [far_spec(position) for position in range(4)],
            out_specs=pl.BlockSpec((halves, slots, edge, width), lambda g, p, order: (0, g, 0, 0)),
        ),
        compiler_params=pltpu.CompilerParams(dimension_semantics=("arbitrary", "arbitrary")),
    )(order, left, far, far, far, far)


def spread_kernel(source_ref, target_ref, rows_ref, out_ref):
    slots = rows_ref.shape[-1] // BLOCK_EDGE
    q, n = pl.program_id(0), pl.program_id(1)
    row = q * pl.num_programs(1) + source_ref[n]
    out_ref[...] = jnp.zeros_like(out_ref)
    for v in range(slots):
        block = rows_ref[0, 0, :, v * BLOCK_EDGE : (v + 1) * BLOCK_EDGE].astype(jnp.float32)
        target = target_ref[row * slots + v]
        odd = lax.rem(target, 2)
        pair = jnp.concatenate(
            [block * (1 - odd).astype(jnp.float32), block * odd.astype(jnp.float32)], axis=1
        ).astype(out_ref.dtype)
        at = pl.multiple_of((target // 2) * (2 * BLOCK_EDGE), 2 * BLOCK_EDGE)
        out_ref[:, pl.ds(at, 2 * BLOCK_EDGE)] += pair


def spread(rows, source, target, panel_cols):
    halves, count, edge, width = rows.shape
    return pl.pallas_call(
        spread_kernel,
        out_shape=jax.ShapeDtypeStruct((halves * count * edge, panel_cols * edge), rows.dtype),
        grid_spec=pltpu.PrefetchScalarGridSpec(
            num_scalar_prefetch=2,
            grid=(halves, count),
            in_specs=[
                pl.BlockSpec((1, 1, edge, width), lambda q, n, source, target: (q, source[n], 0, 0))
            ],
            out_specs=pl.BlockSpec(
                (edge, panel_cols * edge), lambda q, n, source, target: (q * count + n, 0)
            ),
        ),
        compiler_params=pltpu.CompilerParams(dimension_semantics=("arbitrary", "arbitrary")),
    )(source, target, rows)


def band_index(m, row_residue, col_residue, slots):
    first = m - slots // 2 + (col_residue < row_residue).astype(jnp.int32)
    v = jnp.arange(slots, dtype=jnp.int32)
    first = first[..., None]
    return first + (v - first) % slots


def widen(values, index, slots):
    high = (index % (2 * slots)) >= slots
    high = jnp.repeat(high, BLOCK_EDGE, axis=-1)[..., None, :]
    zero = jnp.zeros((), values.dtype)
    return jnp.concatenate(
        [jnp.where(high, zero, values), jnp.where(high, values, zero)], axis=-1
    )


def shards(x_vals, occupancy, perm):
    row_devices = lax.axis_size("row")
    panels = lax.axis_size("col")
    own_row = lax.axis_index("row")
    own_col = lax.axis_index("col")
    local_rows, band_extent, block_area = x_vals.shape
    block_count = perm.shape[0]
    panel_cols = block_count // panels
    halves = panels // row_devices
    slots = band_extent // panels
    lanes = slots * BLOCK_EDGE

    panel_of_residue = perm[:panels] // panel_cols
    residue_ids = jnp.arange(panels, dtype=jnp.int32)
    order = jnp.sum(
        jnp.where(panel_of_residue[None, :] == residue_ids[:, None], residue_ids[None, :], 0), axis=1
    ).astype(jnp.int32)
    inside = perm[::panels] % panel_cols
    m_ids = jnp.arange(panel_cols, dtype=jnp.int32)
    source = jnp.sum(
        jnp.where(inside[None, :] == m_ids[:, None], m_ids[None, :], 0), axis=1
    ).astype(jnp.int32)
    own_residue = order[own_col]
    row_residues = lax.dynamic_slice_in_dim(order, own_row * halves, halves)

    first_row = (own_row * panels + own_col) * local_rows
    row_ids = first_row + jnp.arange(local_rows, dtype=jnp.int32)
    cols = (
        row_ids[:, None] - band_extent // 2 + jnp.arange(band_extent, dtype=jnp.int32)[None, :]
    ) % block_count
    placed = (
        (occupancy[:, :, None, None] == 1)
        & ((cols % panels)[:, :, None, None] == order[None, None, :, None])
        & (
            ((cols // panels) % slots)[:, :, None, None]
            == jnp.arange(slots, dtype=jnp.int32)[None, None, None, :]
        )
    ).astype(jnp.bfloat16)
    kept = jnp.sum(placed.astype(jnp.float32), axis=1).astype(jnp.bfloat16)
    every_kept = lax.all_gather(
        kept.reshape(local_rows, panels * slots), ("row", "col"), axis=0, tiled=True
    ).reshape(panel_cols, panels, panels, slots)
    values = jnp.einsum(
        "kspt,ksf->pktf", placed, x_vals, preferred_element_type=jnp.float32
    ).astype(jnp.bfloat16)
    values = (
        values.reshape(panels, local_rows, slots, BLOCK_EDGE, BLOCK_EDGE)
        .transpose(0, 1, 3, 2, 4)
        .reshape(panels, local_rows, BLOCK_EDGE, lanes)
    )
    first = lax.all_to_all(values, "col", split_axis=0, concat_axis=0, tiled=True)
    first = first.reshape(panels * local_rows, BLOCK_EDGE, lanes)
    far = lax.all_gather(first, "row", axis=0, tiled=True).reshape(
        panel_cols, panels, BLOCK_EDGE, lanes
    )
    tile = jnp.stack(
        [
            lax.dynamic_index_in_dim(far, row_residues[q], axis=1, keepdims=False)
            for q in range(halves)
        ]
    )
    own_kept = lax.dynamic_index_in_dim(every_kept, own_col, axis=2, keepdims=False)
    wanted = jnp.stack(
        [
            lax.dynamic_index_in_dim(own_kept, row_residues[q], axis=1, keepdims=False)
            for q in range(halves)
        ]
    )
    wanted = wanted > 0
    left = lax.all_gather(tile[None], "col", axis=0, tiled=True)

    far_index = band_index(m_ids[:, None], residue_ids[None, :], own_residue, slots)
    far_wide = widen(far, far_index, slots)
    left_index = band_index(
        m_ids[None, None, :], row_residues[None, :, None], order[:, None, None], slots
    )
    left_wide = widen(left, left_index, slots)
    tile_index = band_index(m_ids[None, :], row_residues[:, None], own_residue, slots)
    tile_high = (tile_index % (2 * slots)) >= slots

    def spread_mask(mask):
        return jnp.repeat(mask, BLOCK_EDGE, axis=-1)[:, :, None, :]

    def narrow(wide):
        chosen = jnp.where(spread_mask(tile_high), wide[..., lanes:], wide[..., :lanes])
        return jnp.where(spread_mask(wanted), chosen, 0.0)

    square = narrow(banded_product(left_wide, far_wide, order, False, slots)).astype(jnp.bfloat16)
    far_square = lax.all_gather(square, "row", axis=0, tiled=True)
    square_index = band_index(m_ids[None, :], order[:, None], own_residue, slots)
    square_wide = widen(far_square, square_index, slots)
    cube = narrow(banded_product(left_wide, square_wide, residue_ids, True, slots))
    stepped = (
        1.5 * tile.astype(jnp.float32) - 0.5 / (BLOCK_EDGE * band_extent) * cube
    ).astype(jnp.bfloat16)
    hit = (tile_index % panel_cols)[..., None] == m_ids
    target = jnp.sum(jnp.where(hit, inside, 0), axis=-1).astype(jnp.int32).reshape(-1)
    return spread(stepped, source, target, panel_cols)


def solution(mesh):
    return jax.shard_map(
        shards,
        mesh=mesh,
        in_specs=(P(("row", "col"), None, None), P(("row", "col"), None), P()),
        out_specs=P("row", "col"),
        check_vma=False,
    )
```

time: 2960 us -> 677 us (0.23)
  local copies, waits for them, and re-layouts: 2210 us -> 33.6 us
  matrix products: 268 us -> 2.03 us
  Pallas kernels: 0 us -> 162 us
  blocking collectives: 33.6 us -> 127 us
  waiting for transfers between devices: 331 us -> 246 us
  other arithmetic: 42.8 us -> 83.2 us
    broadcast_in_dim x128 -> x10, local copies, waits for them, and re-layouts: 853 us -> 2.85 us  [the longest x3 1.39 us: widen(): high = jnp.repeat(high, BLOCK_EDGE, axis=-1)[..., None, :]]
    slice x32 -> x2, local copies, waits for them, and re-layouts: 759 us -> 0.7 us  [the longest x1 0.58 us: shards(): row_residues[q]]
    gather x34 -> x0, local copies, waits for them, and re-layouts: 272 us -> none  [the longest x16 258 us: one_group(): whole_rows = far_vals[source]]
    dot_general x24 -> x1, matrix products: 268 us -> 2.03 us  [shards(): jnp.einsum('kspt,ksf->pktf', placed, x_vals, preferred_element_type=jnp.f...]
    pallas_call x0 -> x3, Pallas kernels: none -> 162 us  [the longest x2 126 us: banded_product(): pl.pallas_call(multiply_kernel, out_shape=jax.ShapeDtypeStruct((halves, c...]
    another operation x19 -> x1, local copies, waits for them, and re-layouts: 118 us -> 1.73 us  [shards(): jnp.stack([lax.dynamic_index_in_dim(far, row_residues[q], axis=1, keepdim...]
    all_to_all x3 -> x0, waiting for transfers between devices: 76.4 us -> none  [the longest x1 47.9 us: shards(): lax.all_to_all(values, 'col', split_axis=0, concat_axis=0, tiled=True)]
    dynamic_slice x16 -> x2, local copies, waits for them, and re-layouts: 72.1 us -> 0.82 us  [the longest x1 0.62 us: shards(): own_residue = order[own_col]]
  transfers between devices with their start and end apart: 6 -> 3, of which waited for: 6 -> 3; matrix products, arithmetic and copies ran while one was open for 2% -> 3% of each run, Pallas kernels for 0% -> 0%
where the time goes in v1:
time: 677 us; the launch traced here: 670 us
  waiting for transfers between devices  246 us (36%)
  Pallas kernels  162 us (24%)
  blocking collectives  127 us (19%)
  other arithmetic  83.2 us (12%)
  local copies, waits for them, and re-layouts  33.6 us (5%)
  between operations  17 us (3%)
    all_gather x1, waiting for transfers between devices, shards(): left = lax.all_gather(tile[None], 'col', axis=0, tiled=True)  141 us
    pallas_call x2, Pallas kernels, banded_product(): pl.pallas_call(multiply_kernel, out_shape=jax.ShapeDtypeStruct((halves, c...  126 us
    all_gather x1, blocking collectives, shards(): lax.all_gather(kept.reshape(local_rows, panels * slots), ('row', 'col'),...  71.1 us
    all_to_all x1, blocking collectives, shards(): lax.all_to_all(values, 'col', split_axis=0, concat_axis=0, tiled=True)  55.4 us
    all_gather x1, waiting for transfers between devices, shards(): far_square = lax.all_gather(square, 'row', axis=0, tiled=True)  53.2 us
    all_gather x1, waiting for transfers between devices, shards(): lax.all_gather(first, 'row', axis=0, tiled=True)  51.8 us
    concatenate x3, other arithmetic, widen(): jnp.concatenate([jnp.where(high, zero, values), jnp.where(high, values, z...  36.2 us
    pallas_call x1, Pallas kernels, spread(): pl.pallas_call(spread_kernel, out_shape=jax.ShapeDtypeStruct((halves * co...  35.3 us
  transfers between devices with their start and end apart: 3, of which 3 were waited for; matrix products, arithmetic and copies ran while one was open for 3% of the time, Pallas kernels for 0%

profile of v1, /device:TPU:0, one launch (start us, length us, event | category | flops | bytes accessed | tf_op | source)
XLA Modules:
  0.0 669.9 jit_solution(13469583311150154104)
XLA Ops:
  6.5 0.8 and_select_fusion
  7.6 0.7 broadcast_compare_fusion
  8.4 2.0 fusion
  10.4 6.9 %reshape.322 = bf16[8,8,4,64,64]{4,3,0,2,1:T(8,128)(2,1)} reshape(bf16[8,8,4,4096]{3,0,2,1:T(8,128)(2,1)} %fusion) | data formatting | bytes 4194304 | tf_op jit(solution)/shard_map/reshape | solution.py:158
  17.3 12.4 %copy.23 = bf16[8,8,4,64,64]{4,2,3,1,0:T(4,128)(2,1)} copy(bf16[8,8,4,64,64]{4,3,0,2,1:T(8,128)(2,1)} %reshape.322) | data formatting | bytes 4194304 | tf_op jit(solution)/shard_map/reshape | solution.py:158
  29.7 6.0 reshape.323
  35.7 55.4 %all_to_all.5 = bf16[8,8,64,256]{3,2,1,0:T(8,128)(2,1)} all-to-all(bf16[8,8,64,256]{3,2,1,0:T(8,128)(2,1)S(1)} %reshape.323), channel_id=1, replica_groups=mesh['row'=4,'col'=8] {'col'}, dimensions={0} | all-to-all | bytes 4194304 | tf_op jit(solution)/shard_map/all_to_all | solution.py:162
  91.2 0.6 dynamic_slice.22
  91.9 0.7 compare_convert_fusion.3
  92.6 0.6 fusion.44
  96.8 51.8 %all-gather.5.cloned.1.call-done = bf16[256,64,256]{2,1,0:T(8,128)(2,1)} async-done(((bf16[64,64,256]{2,1,0:T(8,128)(2,1)}), bf16[256,64,256]{2,1,0:T(8,128)(2,1)}) %all-gather.5.cloned.1.call-update) | async-done | bytes 8388624 | tf_op jit(solution)/shard_map/all_gather | solution.py:164
  148.6 1.7 dynamic-slice_bitcast_fusion.1
  150.4 1.7 pad_maximum_fusion.3
  152.6 0.7 broadcast_in_dim.193
  153.8 0.6 compare_convert_fusion.1
  155.6 71.1 %all_gather.13 = bf16[256,32]{1,0:T(8,128)(2,1)S(1)} all-gather(bf16[8,32]{1,0:T(8,128)(2,1)S(1)} %copy.17), channel_id=1, replica_groups=mesh['row'=4,'col'=8] {'row','col'}, dimensions={0}, use_global_device_ids=true | all-gather | bytes 16896 | tf_op jit(solution)/shard_map/all_gather | solution.py:151
  228.2 4.5 broadcast_select_fusion.3
  232.7 6.7 %pad_maximum_fusion.1.far0.far1.far2.far3 = bf16[32,8,64,512]{3,2,1,0:T(8,128)(2,1)} fusion(bf16[32,8,64,256]{3,2,1,0:T(8,128)(2,1)S(1)} %get-tuple-element.14, bf16[32,8,64,256]{3,2,1,0:T(8,128)(2,1)S(1)} %get-tuple-element.13), kind=kLoop, calls=%fused_computation.1 | loop fusion | flops 33554432 | bytes 33554432 | tf_op jit(solution)/shard_map/concatenate | solution.py:107
  239.4 140.6 %all-gather.9.cloned.1.call-done = bf16[16,32,64,256]{3,2,1,0:T(8,128)(2,1)} async-done(((bf16[2,32,64,256]{3,2,1,0:T(8,128)(2,1)}), bf16[16,32,64,256]{3,2,1,0:T(8,128)(2,1)}) %all-gather.9.cloned.1.call-update) | async-done | bytes 16777232 | tf_op jit(solution)/shard_map/all_gather | solution.py:181
  380.0 18.3 %broadcast_select_fusion.1 = (bf16[8,2,32,64,256]{4,3,2,1,0:T(8,128)(2,1)}, bf16[8,2,32,64,256]{4,3,2,1,0:T(8,128)(2,1)}) fusion(bf16[8,2,32,64,256]{4,3,2,1,0:T(8,128)(2,1)} %bitcast.29, pred[8,2,32,256]{3,2,1,0:T(8,128)(4,1)S(1)} %broadcast_in_dim.194), kind=kLoop, calls=%fused_computation.4 | loop fusion | flops 16777216 | bytes 50462720 | tf_op jit(solution)/shard_map/jit(_where)/select_n | solution.py:108
  398.3 22.8 %pad_maximum_fusion.left_ref = bf16[8,2,32,64,512]{4,3,2,1,0:T(8,128)(2,1)} fusion(bf16[8,2,32,64,256]{4,3,2,1,0:T(8,128)(2,1)} %get-tuple-element.10, bf16[8,2,32,64,256]{4,3,2,1,0:T(8,128)(2,1)} %get-tuple-element.9), kind=kLoop, calls=%fused_computation | loop fusion | flops 67108864 | bytes 67108864 | tf_op jit(solution)/shard_map/concatenate | solution.py:107
  421.1 63.3 %shard_map.37 = f32[2,32,64,512]{3,2,1,0:T(8,128)} custom-call(s32[8]{0:T(128)} %copy-done.3, bf16[8,2,32,64,512]{4,3,2,1,0:T(8,128)(2,1)} %pad_maximum_fusion.left_ref, bf16[32,8,64,512]{3,2,1,0:T(8,128)(2,1)} %pad_maximum_fusion.1.far0.far1.far2.far3, bf16[32,8,64,512]{3,2,1,0:T(8,128)(2,1)} %pad_maximum_fusion.1.far0.far1.far2.far3, ...), custom_call_target="tpu_custom_call" | custom-call | tf_op jit(solution)/shard_map/pallas_call | solution.py:43
  484.4 6.4 fusion.6
  490.9 0.6 compare_convert_fusion.2
  492.9 0.7 reshape.321.target_ref
  493.6 0.6 select_reduce_fusion.1.source_ref
  494.2 53.2 %all-gather.7.cloned.1.call-done = bf16[8,32,64,256]{3,2,1,0:T(8,128)(2,1)} async-done(((bf16[2,32,64,256]{3,2,1,0:T(8,128)(2,1)}), bf16[8,32,64,256]{3,2,1,0:T(8,128)(2,1)}) %all-gather.7.cloned.1.call-update) | async-done | bytes 8388624 | tf_op jit(solution)/shard_map/all_gather | solution.py:200
  547.4 4.5 broadcast_select_fusion.5
  551.9 6.7 %pad_maximum_fusion.2.far0.far1.far2.far3 = bf16[8,32,64,512]{3,2,1,0:T(8,128)(2,1)} fusion(bf16[8,32,64,256]{3,2,1,0:T(8,128)(2,1)S(1)} %get-tuple-element.12, bf16[8,32,64,256]{3,2,1,0:T(8,128)(2,1)S(1)} %get-tuple-element.11), kind=kLoop, calls=%fused_computation.2 | loop fusion | flops 33554432 | bytes 33554432 | tf_op jit(solution)/shard_map/concatenate | solution.py:107
  559.2 63.2 %shard_map.38 = f32[2,32,64,512]{3,2,1,0:T(8,128)} custom-call(s32[8]{0:T(128)} %iota.69.order_ref, bf16[8,2,32,64,512]{4,3,2,1,0:T(8,128)(2,1)} %pad_maximum_fusion.left_ref, bf16[8,32,64,512]{3,2,1,0:T(8,128)(2,1)} %pad_maximum_fusion.2.far0.far1.far2.far3, bf16[8,32,64,512]{3,2,1,0:T(8,128)(2,1)} %pad_maximum_fusion.2.far0.far1.far2.far3, ...), custom_call_target="tpu_custom_call" | custom-call | tf_op jit(solution)/shard_map/pallas_call | solution.py:43
  622.4 5.6 fusion.4.rows_ref
  628.0 35.3 %shard_map.39 = bf16[4096,2048]{1,0:T(8,128)(2,1)} custom-call(s32[32]{0:T(128)} %select_reduce_fusion.1.source_ref, s32[256]{0:T(256)} %reshape.321.target_ref, bf16[2,32,64,256]{3,2,1,0:T(8,128)(2,1)} %fusion.4.rows_ref), custom_call_target="tpu_custom_call" | custom-call | tf_op jit(solution)/shard_map/pallas_call | solution.py:79
  (57 shorter events, 6.0 us)
Async XLA Ops:
  6.5 1.9 copy-start
  6.5 142.1 %all-gather.5.cloned.1.call-start = ((), (), s32[]{:S(2)}) async-start(), calls=%async_computation.1 | async-start | bytes 10485760 | tf_op jit(solution)/shard_map/all_gather | solution.py:164
  7.5 144.6 %copy-start.3 = (s32[8]{0:T(128)}, s32[8]{0:T(128)S(1)}, u32[]{:S(2)}) copy-start(s32[8]{0:T(128)S(1)} %select_reduce_fusion.2.order_ref) | copy-start | bytes 100
  91.2 288.9 %all-gather.9.cloned.1.call-start = ((), (), s32[]{:S(2)}) async-start(), calls=%async_computation.3 | async-start | bytes 18874368 | tf_op jit(solution)/shard_map/all_gather | solution.py:181
  150.3 82.4 %copy-start.2 = (bf16[1,32,64,256]{3,2,1,0:T(8,128)(2,1)}, bf16[1,32,64,256]{3,2,1,0:T(8,128)(2,1)S(1)}, u32[]{:S(2)}) copy-start(bf16[1,32,64,256]{3,2,1,0:T(8,128)(2,1)S(1)} %get-tuple-element.16) | copy-start | bytes 3145732
  152.0 395.4 %all-gather.7.cloned.1.call-start = ((), (), s32[]{:S(2)}) async-start(), calls=%async_computation.2 | async-start | bytes 10485760 | tf_op jit(solution)/shard_map/all_gather | solution.py:200
  484.4 6.4 copy-start.5
  484.4 6.6 copy-start.4
  622.4 40.9 %copy-start.1 = (bf16[8,32,4096]{2,1,0:T(8,128)(2,1)S(1)}, bf16[8,32,4096]{2,1,0:T(8,128)(2,1)}, u32[]{:S(2)}) copy-start(bf16[8,32,4096]{2,1,0:T(8,128)(2,1)} %param.3) | copy-start | bytes 6291460
Sparse Core Ops, SparseCore 0:
  91.3 57.2 all-gather.4
  152.2 227.8 all-gather.8
  490.9 56.4 all-gather.6
